TPU v7x, 128 devices: a whole 4x4x4 slice. The times are simulated.
128 devices in a mesh: segment: 4 (over x), col: 32 (over z, y, core).
Axes of the slice: x: 4, y: 4, z: 4, core: 2. Of those that a mesh axis runs over, the one named last changes fastest.
Arguments:
- left_env: bfloat16 [384, 8192], P(None, 'col'), may hold values from -6 to 6
- bit_strings: int32 [384, 4], P(None, 'segment'), may hold values from 0 to 1
- site_tensors: bfloat16 [4, 2, 8192, 8192], P('segment', None, None, 'col'), may hold values from -0.0625 to 0.0625
Outputs:
- section_env: bfloat16 [4, 384, 8192], P('segment', None, 'col')
- section_log: float32 [4, 384], P('segment')
All inputs are finite; a program needn't handle non-finite values. Where the computation divides by a largest or mean magnitude, that divisor is 1e-20 or more.
Results may differ from a plain program's by a relative error of at most 0.0065.
Values may be sent and summed in bfloat16 or wider, within the bound.
No kernel may reach another device: no remote copies, remote signals or barrier semaphores. Data moves between devices by JAX's collectives and lax.ppermute only.
A program may use at most 128 MiB of HBM per device.

v0:
```python
import jax
import jax.numpy as jnp
from jax import lax
from jax.sharding import PartitionSpec as P

MICRO = 2
epsilon = 1e-06


def sent_to_all(value, axis):
    length = lax.axis_size(axis)
    return lax.all_to_all(
        jnp.broadcast_to(value[None], (length, *value.shape)), axis, 0, 0, tiled=True
    )


def taken_together(value, axis):
    everything = sent_to_all(value, axis)
    return jnp.max(everything, axis=0)


def passed_along(value, axis, by):
    length = lax.axis_size(axis)
    pairs = [(i, i + by) for i in range(length) if 0 <= i + by < length]
    return lax.ppermute(value, axis, pairs)


def advance(vector, bit_column, tensor):
    batch_rows = vector.shape[0]
    col_width = tensor.shape[2]
    block = min(128, batch_rows)
    buffer_rows = (batch_rows + block - 1 + block - 1) // block * block
    block_count = buffer_rows // block
    ones_before = jnp.cumsum(bit_column) - bit_column
    index_rows = jnp.arange(batch_rows, dtype=jnp.int32)
    zeros_before = index_rows - ones_before
    zero_count = batch_rows - jnp.sum(bit_column)
    start_one = (zero_count + block - 1) // block * block
    slot = jnp.where(bit_column == 1, start_one + ones_before, zeros_before)
    source = jnp.zeros((buffer_rows,), jnp.int32).at[slot].set(index_rows)
    filled = jnp.zeros((buffer_rows,), jnp.bool_).at[slot].set(True)
    block_bit = (jnp.arange(block_count, dtype=jnp.int32) * block >= start_one).astype(jnp.int32)
    arranged_in = jnp.where(
        filled[:, None], jnp.take(vector, source, axis=0), jnp.zeros((), vector.dtype)
    )
    gathered_piece = lax.all_gather(arranged_in, "col", axis=1, tiled=True)
    width = gathered_piece.shape[1]
    pieces = gathered_piece.reshape(block_count, block, width)

    def one_block(inputs):
        rows_block, bit_value = inputs
        weight_block = lax.dynamic_slice(
            tensor, (bit_value, 0, jnp.int32(0)), (1, width, col_width)
        )[0]
        return jnp.dot(rows_block, weight_block, preferred_element_type=jnp.float32)

    result = lax.map(one_block, (pieces, block_bit))
    arranged_out = result.reshape(buffer_rows, col_width)
    chosen = jnp.take(arranged_out, slot, axis=0)
    maximum = taken_together(jnp.max(jnp.abs(chosen), axis=1), "col") + epsilon
    return ((chosen / maximum[:, None]).astype(jnp.bfloat16), jnp.log(maximum))


def local(left_env, bit_strings, site_tensors):
    segment_count = lax.axis_size("segment")
    segment_index = lax.axis_index("segment")
    row_count = left_env.shape[0]
    col_width = left_env.shape[1]
    granules = MICRO
    batch_rows = row_count // granules
    env_out = jnp.zeros((row_count, col_width), jnp.bfloat16)
    log_out = jnp.zeros((row_count,), jnp.float32)
    incoming = jnp.zeros((batch_rows, col_width), jnp.bfloat16)
    tick_total = granules + segment_count - 1
    for tick_step in range(tick_total):
        position = tick_step - segment_index
        active = (position >= 0) & (position < granules)
        offset_rows = jnp.clip(position, 0, granules - 1) * batch_rows
        from_input = lax.dynamic_slice_in_dim(left_env, offset_rows, batch_rows, 0)
        current = jnp.where(segment_index == 0, from_input, incoming)
        bit_block = lax.dynamic_slice_in_dim(bit_strings, offset_rows, batch_rows, 0)
        current, logs_site = advance(current, bit_block[:, 0], site_tensors[0])
        old_env = lax.dynamic_slice_in_dim(env_out, offset_rows, batch_rows, 0)
        old_log = lax.dynamic_slice_in_dim(log_out, offset_rows, batch_rows, 0)
        env_out = lax.dynamic_update_slice_in_dim(
            env_out, jnp.where(active, current, old_env), offset_rows, 0
        )
        log_out = lax.dynamic_update_slice_in_dim(
            log_out, jnp.where(active, logs_site, old_log), offset_rows, 0
        )
        if tick_step + 1 < tick_total:
            incoming = passed_along(current, "segment", 1)
    return (env_out[None], log_out[None])


def solution(mesh):
    placed = (P(None, "col"), P(None, "segment"), P("segment", None, None, "col"))
    return jax.shard_map(
        local,
        mesh=mesh,
        in_specs=placed,
        out_specs=(P("segment", None, "col"), P("segment", None)),
        check_vma=False,
    )
```

profile of v0, /device:TPU:1, one launch (start us, length us, event | category | flops | bytes accessed | tf_op | source)
XLA Modules:
  0.0 496.4 jit_solution(4290405413867485066)
XLA Ops:
  7.2 1.7 fusion.101
  10.3 1.2 scatter_custom_fusion.1
  11.5 0.9 dynamic-slice_select_fusion.4
  12.4 2.1 gather_fusion
  14.5 1.2 scatter_custom_fusion
  19.2 1.2 scatter_custom_fusion.3
  20.4 54.5 %all-gather.6.cloned.1.call-done = bf16[384,8192]{1,0:T(8,128)(2,1)} async-done(((bf16[384,256]{1,0:T(8,128)(2,1)}), bf16[384,8192]{1,0:T(8,128)(2,1)}) %all-gather.6.cloned.1.call-update) | async-done | bytes 6291472 | tf_op jit(solution)/shard_map/all_gather | solution.py:46
  75.0 18.3 %while.50 = (s32[]{:T(128)}, f32[3,128,256]{2,1,0:T(8,128)S(1)}, bf16[3,128,8192]{2,1,0:T(8,128)(2,1)}, s32[3]{0:T(128)S(1)}, bf16[2,8192,256]{2,1,0:T(8,128)(2,1)}, /*index=5*/s32[]{:T(128)}, s32[]{:T(128)}, s32[]{:T(128)}) while((s32[]{:T(128)}, f32[3,128,256]{2,1,0:T(8,128)S(1)}, bf16[3,128,8192]{2,1,0:T(8,128)(2,1)}, s32[3]{0:T(128)S(1)}, ...), condition=%wide.region_6.8_spmd, body=%wide.region_5.7_spmd.sunk | while | flops 536870912 | bytes 6423687 | solution.py:57
  77.5 3.5 fusion.123
  83.6 3.5 fusion.123
  89.7 3.5 fusion.123
  93.3 0.9 gather_fusion.1
  95.0 5.5 %all-to-all-start = ((f32[32,1,192]{2,1,0:T(1,128)}), f32[32,1,192]{2,1,0:T(1,128)S(1)}, u32[]{:S(2)}, u32[]{:S(2)}) async-start(f32[32,1,192]{2,1,0:T(1,128)} %broadcast_in_dim.147), calls=%async_computation | async-start | bytes 65536 | tf_op jit(solution)/shard_map/all_to_all | solution.py:12
  100.6 1.2 scatter_custom_fusion.2
  101.8 5.9 %all-to-all-done = f32[32,1,192]{2,1,0:T(1,128)S(1)} async-done(((f32[32,1,192]{2,1,0:T(1,128)}), f32[32,1,192]{2,1,0:T(1,128)S(1)}, u32[]{:S(2)}, u32[]{:S(2)}) %all-to-all-start) | async-done | bytes 24608 | tf_op jit(solution)/shard_map/all_to_all | solution.py:12
  108.1 3.1 collective-permute-start
  111.2 1.6 collective-permute-done
  112.8 2.1 gather_fusion.2
  115.8 1.2 scatter_custom_fusion.5
  117.0 53.0 %all-gather.8.cloned.1.call-done = bf16[384,8192]{1,0:T(8,128)(2,1)} async-done(((bf16[384,256]{1,0:T(8,128)(2,1)}), bf16[384,8192]{1,0:T(8,128)(2,1)}) %all-gather.8.cloned.1.call-update) | async-done | bytes 6291472 | tf_op jit(solution)/shard_map/all_gather | solution.py:46
  170.1 18.3 %while.51 = (s32[]{:T(128)}, f32[3,128,256]{2,1,0:T(8,128)S(1)}, bf16[3,128,8192]{2,1,0:T(8,128)(2,1)}, s32[3]{0:T(128)S(1)}, bf16[2,8192,256]{2,1,0:T(8,128)(2,1)}, /*index=5*/s32[]{:T(128)}, s32[]{:T(128)}, s32[]{:T(128)}) while((s32[]{:T(128)}, f32[3,128,256]{2,1,0:T(8,128)S(1)}, bf16[3,128,8192]{2,1,0:T(8,128)(2,1)}, s32[3]{0:T(128)S(1)}, ...), condition=%wide.region_15.18_spmd, body=%wide.region_14.17_spmd.sunk | while | flops 536870912 | bytes 6423687 | solution.py:57
  172.6 3.5 fusion.126
  178.7 3.5 fusion.126
  184.8 3.5 fusion.126
  188.4 0.9 gather_fusion.3
  190.1 5.5 %all-to-all-start.1 = ((f32[32,1,192]{2,1,0:T(1,128)}), f32[32,1,192]{2,1,0:T(1,128)S(1)}, u32[]{:S(2)}, u32[]{:S(2)}) async-start(f32[32,1,192]{2,1,0:T(1,128)} %broadcast_in_dim.150), calls=%async_computation.1 | async-start | bytes 65536 | tf_op jit(solution)/shard_map/all_to_all | solution.py:12
  195.7 1.2 scatter_custom_fusion.4
  196.9 5.9 %all-to-all-done.1 = f32[32,1,192]{2,1,0:T(1,128)S(1)} async-done(((f32[32,1,192]{2,1,0:T(1,128)}), f32[32,1,192]{2,1,0:T(1,128)S(1)}, u32[]{:S(2)}, u32[]{:S(2)}) %all-to-all-start.1) | async-done | bytes 24608 | tf_op jit(solution)/shard_map/all_to_all | solution.py:12
  203.2 3.3 collective-permute-start.1
  206.5 1.4 collective-permute-done.1
  208.0 2.1 gather_fusion.4
  213.4 1.2 scatter_custom_fusion.7
  214.7 50.5 %all-gather.10.cloned.1.call-done = bf16[384,8192]{1,0:T(8,128)(2,1)} async-done(((bf16[384,256]{1,0:T(8,128)(2,1)}), bf16[384,8192]{1,0:T(8,128)(2,1)}) %all-gather.10.cloned.1.call-update) | async-done | bytes 6291472 | tf_op jit(solution)/shard_map/all_gather | solution.py:46
  265.2 18.3 %while.52 = (s32[]{:T(128)}, f32[3,128,256]{2,1,0:T(8,128)S(1)}, bf16[3,128,8192]{2,1,0:T(8,128)(2,1)}, s32[3]{0:T(128)S(1)}, bf16[2,8192,256]{2,1,0:T(8,128)(2,1)}, /*index=5*/s32[]{:T(128)}, s32[]{:T(128)}, s32[]{:T(128)}) while((s32[]{:T(128)}, f32[3,128,256]{2,1,0:T(8,128)S(1)}, bf16[3,128,8192]{2,1,0:T(8,128)(2,1)}, s32[3]{0:T(128)S(1)}, ...), condition=%wide.region_24.27_spmd, body=%wide.region_23.26_spmd.sunk | while | flops 536870912 | bytes 6423687 | solution.py:57
  267.8 3.5 fusion.129
  273.9 3.5 fusion.129
  280.0 3.5 fusion.129
  283.5 0.9 gather_fusion.5
  285.2 5.5 %all-to-all-start.2 = ((f32[32,1,192]{2,1,0:T(1,128)}), f32[32,1,192]{2,1,0:T(1,128)S(1)}, u32[]{:S(2)}, u32[]{:S(2)}) async-start(f32[32,1,192]{2,1,0:T(1,128)} %broadcast_in_dim.153), calls=%async_computation.2 | async-start | bytes 65536 | tf_op jit(solution)/shard_map/all_to_all | solution.py:12
  290.8 1.2 scatter_custom_fusion.6
  292.1 5.9 %all-to-all-done.2 = f32[32,1,192]{2,1,0:T(1,128)S(1)} async-done(((f32[32,1,192]{2,1,0:T(1,128)}), f32[32,1,192]{2,1,0:T(1,128)S(1)}, u32[]{:S(2)}, u32[]{:S(2)}) %all-to-all-start.2) | async-done | bytes 24608 | tf_op jit(solution)/shard_map/all_to_all | solution.py:12
  298.4 3.1 collective-permute-start.2
  301.5 1.6 collective-permute-done.2
  303.1 2.1 gather_fusion.6
  306.1 1.2 scatter_custom_fusion.9
  307.3 53.0 %all-gather.12.cloned.1.call-done = bf16[384,8192]{1,0:T(8,128)(2,1)} async-done(((bf16[384,256]{1,0:T(8,128)(2,1)}), bf16[384,8192]{1,0:T(8,128)(2,1)}) %all-gather.12.cloned.1.call-update) | async-done | bytes 6291472 | tf_op jit(solution)/shard_map/all_gather | solution.py:46
  360.4 18.3 %while.53 = (s32[]{:T(128)}, f32[3,128,256]{2,1,0:T(8,128)S(1)}, bf16[3,128,8192]{2,1,0:T(8,128)(2,1)}, s32[3]{0:T(128)S(1)}, bf16[2,8192,256]{2,1,0:T(8,128)(2,1)}, /*index=5*/s32[]{:T(128)}, s32[]{:T(128)}, s32[]{:T(128)}) while((s32[]{:T(128)}, f32[3,128,256]{2,1,0:T(8,128)S(1)}, bf16[3,128,8192]{2,1,0:T(8,128)(2,1)}, s32[3]{0:T(128)S(1)}, ...), condition=%wide.region_33.36_spmd, body=%wide.region_32.35_spmd.sunk | while | flops 536870912 | bytes 6423687 | solution.py:57
  362.9 3.5 fusion.132
  369.0 3.5 fusion.132
  375.1 3.5 fusion.132
  380.4 5.5 %all-to-all-start.3 = ((f32[32,1,192]{2,1,0:T(1,128)}), f32[32,1,192]{2,1,0:T(1,128)S(1)}, u32[]{:S(2)}, u32[]{:S(2)}) async-start(f32[32,1,192]{2,1,0:T(1,128)} %broadcast_in_dim.156), calls=%async_computation.3 | async-start | bytes 65536 | tf_op jit(solution)/shard_map/all_to_all | solution.py:12
  386.0 1.2 scatter_custom_fusion.8
  387.2 5.9 %all-to-all-done.3 = f32[32,1,192]{2,1,0:T(1,128)S(1)} async-done(((f32[32,1,192]{2,1,0:T(1,128)}), f32[32,1,192]{2,1,0:T(1,128)S(1)}, u32[]{:S(2)}, u32[]{:S(2)}) %all-to-all-start.3) | async-done | bytes 24608 | tf_op jit(solution)/shard_map/all_to_all | solution.py:12
  393.5 3.1 collective-permute-start.3
  396.6 1.6 collective-permute-done.3
  398.3 2.1 gather_fusion.8
  401.2 54.3 %all-gather.14.cloned.1.call-done = bf16[384,8192]{1,0:T(8,128)(2,1)} async-done(((bf16[384,256]{1,0:T(8,128)(2,1)}), bf16[384,8192]{1,0:T(8,128)(2,1)}) %all-gather.14.cloned.1.call-update) | async-done | bytes 6291472 | tf_op jit(solution)/shard_map/all_gather | solution.py:46
  455.5 18.3 %while.54 = (s32[]{:T(128)}, f32[3,128,256]{2,1,0:T(8,128)S(1)}, bf16[3,128,8192]{2,1,0:T(8,128)(2,1)}, s32[3]{0:T(128)S(1)}, bf16[2,8192,256]{2,1,0:T(8,128)(2,1)}, /*index=5*/s32[]{:T(128)}, s32[]{:T(128)}, s32[]{:T(128)}) while((s32[]{:T(128)}, f32[3,128,256]{2,1,0:T(8,128)S(1)}, bf16[3,128,8192]{2,1,0:T(8,128)(2,1)}, s32[3]{0:T(128)S(1)}, ...), condition=%wide.region_42.45_spmd, body=%wide.region_41.44_spmd.sunk | while | flops 536870912 | bytes 6423687 | solution.py:57
  458.1 3.5 fusion.135
  464.2 3.5 fusion.135
  470.3 3.5 fusion.135
  473.8 0.9 gather_fusion.9
  475.5 5.5 %all-to-all-start.4 = ((f32[32,1,192]{2,1,0:T(1,128)}), f32[32,1,192]{2,1,0:T(1,128)S(1)}, u32[]{:S(2)}, u32[]{:S(2)}) async-start(f32[32,1,192]{2,1,0:T(1,128)} %broadcast_in_dim.160), calls=%async_computation.4 | async-start | bytes 65536 | tf_op jit(solution)/shard_map/all_to_all | solution.py:12
  481.1 7.2 %all-to-all-done.4 = f32[32,1,192]{2,1,0:T(1,128)S(1)} async-done(((f32[32,1,192]{2,1,0:T(1,128)}), f32[32,1,192]{2,1,0:T(1,128)S(1)}, u32[]{:S(2)}, u32[]{:S(2)}) %all-to-all-start.4) | async-done | bytes 24608 | tf_op jit(solution)/shard_map/all_to_all | solution.py:12
  (140 shorter events, 24.8 us)
Async XLA Ops:
  7.2 67.8 %all-gather.6.cloned.1.call-start = ((), (), s32[]{:S(2)}) async-start(), calls=%async_computation.5 | async-start | bytes 6488064 | tf_op jit(solution)/shard_map/all_gather | solution.py:46
  75.0 37.8 %copy-start = (bf16[384,256]{1,0:T(8,128)(2,1)S(1)}, bf16[384,256]{1,0:T(8,128)(2,1)}, u32[]{:S(2)}) copy-start(bf16[384,256]{1,0:T(8,128)(2,1)} %param.17) | copy-start | bytes 589828
  95.0 12.8 %all-to-all-start = ((f32[32,1,192]{2,1,0:T(1,128)}), f32[32,1,192]{2,1,0:T(1,128)S(1)}, u32[]{:S(2)}, u32[]{:S(2)}) async-start(f32[32,1,192]{2,1,0:T(1,128)} %broadcast_in_dim.147), calls=%async_computation | async-start | bytes 65536 | tf_op jit(solution)/shard_map/all_to_all | solution.py:12
  100.5 69.6 %all-gather.8.cloned.1.call-start = ((), (), s32[]{:S(2)}) async-start(), calls=%async_computation.6 | async-start | bytes 6488064 | tf_op jit(solution)/shard_map/all_gather | solution.py:46
  108.1 4.7 collective-permute-start
  190.1 12.8 %all-to-all-start.1 = ((f32[32,1,192]{2,1,0:T(1,128)}), f32[32,1,192]{2,1,0:T(1,128)S(1)}, u32[]{:S(2)}, u32[]{:S(2)}) async-start(f32[32,1,192]{2,1,0:T(1,128)} %broadcast_in_dim.150), calls=%async_computation.1 | async-start | bytes 65536 | tf_op jit(solution)/shard_map/all_to_all | solution.py:12
  195.6 69.6 %all-gather.10.cloned.1.call-start = ((), (), s32[]{:S(2)}) async-start(), calls=%async_computation.7 | async-start | bytes 6488064 | tf_op jit(solution)/shard_map/all_gather | solution.py:46
  203.2 4.7 collective-permute-start.1
  285.2 12.8 %all-to-all-start.2 = ((f32[32,1,192]{2,1,0:T(1,128)}), f32[32,1,192]{2,1,0:T(1,128)S(1)}, u32[]{:S(2)}, u32[]{:S(2)}) async-start(f32[32,1,192]{2,1,0:T(1,128)} %broadcast_in_dim.153), calls=%async_computation.2 | async-start | bytes 65536 | tf_op jit(solution)/shard_map/all_to_all | solution.py:12
  290.8 69.6 %all-gather.12.cloned.1.call-start = ((), (), s32[]{:S(2)}) async-start(), calls=%async_computation.8 | async-start | bytes 6488064 | tf_op jit(solution)/shard_map/all_gather | solution.py:46
  298.4 4.7 collective-permute-start.2
  380.4 12.8 %all-to-all-start.3 = ((f32[32,1,192]{2,1,0:T(1,128)}), f32[32,1,192]{2,1,0:T(1,128)S(1)}, u32[]{:S(2)}, u32[]{:S(2)}) async-start(f32[32,1,192]{2,1,0:T(1,128)} %broadcast_in_dim.156), calls=%async_computation.3 | async-start | bytes 65536 | tf_op jit(solution)/shard_map/all_to_all | solution.py:12
  385.9 69.6 %all-gather.14.cloned.1.call-start = ((), (), s32[]{:S(2)}) async-start(), calls=%async_computation.9 | async-start | bytes 6488064 | tf_op jit(solution)/shard_map/all_gather | solution.py:46
  393.5 4.7 collective-permute-start.3
  475.5 12.8 %all-to-all-start.4 = ((f32[32,1,192]{2,1,0:T(1,128)}), f32[32,1,192]{2,1,0:T(1,128)S(1)}, u32[]{:S(2)}, u32[]{:S(2)}) async-start(f32[32,1,192]{2,1,0:T(1,128)} %broadcast_in_dim.160), calls=%async_computation.4 | async-start | bytes 65536 | tf_op jit(solution)/shard_map/all_to_all | solution.py:12
  488.6 0.6 copy-start.2
  489.2 0.7 copy-start.1
Sparse Core Ops, SparseCore 0:
  16.7 58.1 all-gather.5
  115.9 54.1 all-gather.7
  211.0 54.1 all-gather.9
  306.2 54.1 all-gather.11
  401.3 54.1 all-gather.13
where the time goes:
time: 497 us; the launch traced here: 496 us
  waiting for transfers between devices  303 us (61%)
  matrix products  53.1 us (11%)
  local copies, waits for them, and re-layouts  41.3 us (8%)
  starting transfers between devices  40.3 us (8%)
  loops' own time  29.5 us (6%)
  between operations  17.7 us (4%)
  other arithmetic  11.8 us (2%)
    all_gather x5, waiting for transfers between devices, advance(): gathered_piece = lax.all_gather(arranged_in, 'col', axis=1, tiled=True)  265 us
    dot_general x15, matrix products, one_block(): return jnp.dot(rows_block, weight_block, preferred_element_type=jnp.float32)  53.1 us
    all_to_all x5, waiting for transfers between devices, sent_to_all(): lax.all_to_all(jnp.broadcast_to(value[None], (length, *value.shape)), axi...  30.9 us
    another operation x5, loops' own time, advance(): result = lax.map(one_block, (pieces, block_bit))  29.5 us
    all_to_all x5, starting transfers between devices, sent_to_all(): lax.all_to_all(jnp.broadcast_to(value[None], (length, *value.shape)), axi...  27.5 us
    ppermute x4, starting transfers between devices, passed_along(): return lax.ppermute(value, axis, pairs)  12.6 us
    gather x5, local copies, waits for them, and re-layouts, advance(): jnp.take(vector, source, axis=0)  10.3 us
  transfers between devices with their start and end apart: 14, of which 14 were waited for; matrix products, arithmetic and copies ran while one was open for 3% of the time, Pallas kernels for 0%

commit v1 on v0

--- a/solution.py
+++ b/solution.py
@@ -1,10 +1,21 @@
+import functools
 import jax
 import jax.numpy as jnp
 from jax import lax
 from jax.sharding import PartitionSpec as P
+from jax.lax import all_to_all, axis_size
 
 MICRO = 2
 epsilon = 1e-06
+
+
+def turns_follow(work_x, chip_axis):
+    now = jnp.stack([work_x] * axis_size(chip_axis), 0)
+    e_now = jnp.concatenate(all_to_all(now, chip_axis, 0, 0), 1)
+    return e_now
+
+
+lift_frames = functools.partial(turns_follow, chip_axis="col")
 
 
 def sent_to_all(value, axis):
@@ -43,7 +54,7 @@
     arranged_in = jnp.where(
         filled[:, None], jnp.take(vector, source, axis=0), jnp.zeros((), vector.dtype)
     )
-    gathered_piece = lax.all_gather(arranged_in, "col", axis=1, tiled=True)
+    gathered_piece = lift_frames(arranged_in)
     width = gathered_piece.shape[1]
     pieces = gathered_piece.reshape(block_count, block, width)
 

time: 497 us -> 748 us (1.51); the launches traced: 496 us -> 737 us
  local copies, waits for them, and re-layouts: 41.3 us -> 156 us
  waiting for transfers between devices: 303 us -> 392 us
  starting transfers between devices: 40.3 us -> 93 us
  between operations: 17.7 us -> 4.94 us
    all_to_all x0 -> x5, waiting for transfers between devices: none -> 354 us  [turns_follow(): e_now = jnp.concatenate(all_to_all(now, chip_axis, 0, 0), 1)]
    all_gather x5 -> x0, waiting for transfers between devices: 265 us -> none  [advance(): gathered_piece = lax.all_gather(arranged_in, 'col', axis=1, tiled=True)]
    another operation x19 -> x29, local copies, waits for them, and re-layouts: 1.02 us -> 70 us  [the longest x5 52.2 us: advance(): pieces = gathered_piece.reshape(block_count, block, width)]
    reshape x1 -> x6, local copies, waits for them, and re-layouts: 0.01 us -> 45 us  [the longest x5 45 us: turns_follow(): e_now = jnp.concatenate(all_to_all(now, chip_axis, 0, 0), 1)]
    all_to_all x0 -> x5, starting transfers between devices: none -> 33.8 us  [turns_follow(): e_now = jnp.concatenate(all_to_all(now, chip_axis, 0, 0), 1)]
    all_to_all x5, starting transfers between devices: 27.5 us -> 43.6 us  [sent_to_all(): lax.all_to_all(jnp.broadcast_to(value[None], (length, *value.shape)), axi...]
  transfers between devices with their start and end apart: 14 -> 14, of which waited for: 14 -> 14; matrix products, arithmetic and copies ran while one was open for 3% -> 2% of each run, Pallas kernels for 0% -> 0%
where the time goes in v1:
time: 748 us; the launch traced here: 737 us
  waiting for transfers between devices  392 us (52%)
  local copies, waits for them, and re-layouts  156 us (21%)
  starting transfers between devices  93 us (12%)
  matrix products  53.1 us (7%)
  loops' own time  29.5 us (4%)
  other arithmetic  8.44 us (1%)
    all_to_all x5, waiting for transfers between devices, turns_follow(): e_now = jnp.concatenate(all_to_all(now, chip_axis, 0, 0), 1)  354 us
    dot_general x15, matrix products, one_block(): return jnp.dot(rows_block, weight_block, preferred_element_type=jnp.float32)  53.1 us
    another operation x5, local copies, waits for them, and re-layouts, advance(): pieces = gathered_piece.reshape(block_count, block, width)  52.2 us
    reshape x5, local copies, waits for them, and re-layouts, turns_follow(): e_now = jnp.concatenate(all_to_all(now, chip_axis, 0, 0), 1)  45 us
    all_to_all x5, starting transfers between devices, sent_to_all(): lax.all_to_all(jnp.broadcast_to(value[None], (length, *value.shape)), axi...  43.6 us
    all_to_all x5, starting transfers between devices, turns_follow(): e_now = jnp.concatenate(all_to_all(now, chip_axis, 0, 0), 1)  33.8 us
    all_to_all x5, waiting for transfers between devices, sent_to_all(): lax.all_to_all(jnp.broadcast_to(value[None], (length, *value.shape)), axi...  31.6 us
    another operation x5, loops' own time, advance(): result = lax.map(one_block, (pieces, block_bit))  29.5 us
  transfers between devices with their start and end apart: 14, of which 14 were waited for; matrix products, arithmetic and copies ran while one was open for 2% of the time, Pallas kernels for 0%

profile of v1, /device:TPU:1, one launch (start us, length us, event | category | flops | bytes accessed | tf_op | source)
XLA Modules:
  0.0 736.9 jit_solution(12527223140972619601)
XLA Ops:
  5.9 2.1 gather_fusion
  9.4 3.4 stack.10
  12.8 9.7 %all-to-all-start = ((bf16[32,384,256]{2,1,0:T(8,128)(2,1)}), bf16[32,384,256]{2,1,0:T(8,128)(2,1)}, u32[]{:S(2)}, u32[]{:S(2)}) async-start(bf16[32,384,256]{2,1,0:T(8,128)(2,1)} %stack.10), calls=%async_computation | async-start | bytes 12582912 | tf_op jit(solution)/shard_map/all_to_all | solution.py:14
  26.2 69.1 %all-to-all-done = bf16[32,384,256]{2,1,0:T(8,128)(2,1)} async-done(((bf16[32,384,256]{2,1,0:T(8,128)(2,1)}), bf16[32,384,256]{2,1,0:T(8,128)(2,1)}, u32[]{:S(2)}, u32[]{:S(2)}) %all-to-all-start) | async-done | bytes 6291488 | tf_op jit(solution)/shard_map/all_to_all | solution.py:14
  95.4 9.0 %copy.15 = bf16[384,32,256]{2,1,0:T(8,128)(2,1)} copy(bf16[384,32,256]{2,0,1:T(8,128)(2,1)} %bitcast.23) | data formatting | bytes 12582912 | tf_op jit(solution)/shard_map/reshape | solution.py:14
  104.4 10.4 %reshape_reshape.15 = bf16[3,128,8192]{2,1,0:T(8,128)(2,1)} reshape(bf16[384,32,256]{2,1,0:T(8,128)(2,1)} %copy.15) | data formatting | bytes 12582912 | tf_op jit(solution)/shard_map/reshape;reshape | solution.py:59
  114.8 18.3 %while.50 = (s32[]{:T(128)}, f32[3,128,256]{2,1,0:T(8,128)S(1)}, bf16[3,128,8192]{2,1,0:T(8,128)(2,1)}, s32[3]{0:T(128)S(1)}, bf16[2,8192,256]{2,1,0:T(8,128)(2,1)}, /*index=5*/s32[]{:T(128)}, s32[]{:T(128)}, s32[]{:T(128)}) while((s32[]{:T(128)}, f32[3,128,256]{2,1,0:T(8,128)S(1)}, bf16[3,128,8192]{2,1,0:T(8,128)(2,1)}, s32[3]{0:T(128)S(1)}, ...), condition=%wide.region_6.8_spmd, body=%wide.region_5.7_spmd.sunk | while | flops 536870912 | bytes 6423687 | solution.py:68
  117.4 3.5 fusion.123
  123.5 3.5 fusion.123
  129.6 3.5 fusion.123
  134.9 8.7 %all-to-all-start.1 = ((f32[32,1,192]{2,1,0:T(1,128)}), f32[32,1,192]{2,1,0:T(1,128)S(1)}, u32[]{:S(2)}, u32[]{:S(2)}) async-start(f32[32,1,192]{2,1,0:T(1,128)} %broadcast_in_dim.147), calls=%async_computation.1 | async-start | bytes 65536 | tf_op jit(solution)/shard_map/all_to_all | solution.py:23
  144.9 6.1 all-to-all-done.1
  151.3 3.3 collective-permute-start
  156.1 2.1 gather_fusion.2
  158.3 3.4 stack.11
  161.7 5.9 all-to-all-start.2
  168.8 71.8 %all-to-all-done.2 = bf16[32,384,256]{2,1,0:T(8,128)(2,1)} async-done(((bf16[32,384,256]{2,1,0:T(8,128)(2,1)}), bf16[32,384,256]{2,1,0:T(8,128)(2,1)}, u32[]{:S(2)}, u32[]{:S(2)}) %all-to-all-start.2) | async-done | bytes 6291488 | tf_op jit(solution)/shard_map/all_to_all | solution.py:14
  240.6 9.0 %copy.17 = bf16[384,32,256]{2,1,0:T(8,128)(2,1)} copy(bf16[384,32,256]{2,0,1:T(8,128)(2,1)} %bitcast.29) | data formatting | bytes 12582912 | tf_op jit(solution)/shard_map/reshape | solution.py:14
  249.6 10.4 %reshape_reshape.16 = bf16[3,128,8192]{2,1,0:T(8,128)(2,1)} reshape(bf16[384,32,256]{2,1,0:T(8,128)(2,1)} %copy.17) | data formatting | bytes 12582912 | tf_op jit(solution)/shard_map/reshape;reshape | solution.py:59
  260.0 18.3 %while.51 = (s32[]{:T(128)}, f32[3,128,256]{2,1,0:T(8,128)S(1)}, bf16[3,128,8192]{2,1,0:T(8,128)(2,1)}, s32[3]{0:T(128)S(1)}, bf16[2,8192,256]{2,1,0:T(8,128)(2,1)}, /*index=5*/s32[]{:T(128)}, s32[]{:T(128)}, s32[]{:T(128)}) while((s32[]{:T(128)}, f32[3,128,256]{2,1,0:T(8,128)S(1)}, bf16[3,128,8192]{2,1,0:T(8,128)(2,1)}, s32[3]{0:T(128)S(1)}, ...), condition=%wide.region_15.18_spmd, body=%wide.region_14.17_spmd.sunk | while | flops 536870912 | bytes 6423687 | solution.py:68
  262.6 3.5 fusion.126
  268.7 3.5 fusion.126
  274.8 3.5 fusion.126
  280.0 8.8 %all-to-all-start.3 = ((f32[32,1,192]{2,1,0:T(1,128)}), f32[32,1,192]{2,1,0:T(1,128)S(1)}, u32[]{:S(2)}, u32[]{:S(2)}) async-start(f32[32,1,192]{2,1,0:T(1,128)} %broadcast_in_dim.150), calls=%async_computation.3 | async-start | bytes 65536 | tf_op jit(solution)/shard_map/all_to_all | solution.py:23
  290.1 6.1 all-to-all-done.3
  296.6 4.1 collective-permute-start.1
  302.3 2.1 gather_fusion.4
  304.6 3.4 stack.12
  307.9 6.2 all-to-all-start.4
  318.0 69.0 %all-to-all-done.4 = bf16[32,384,256]{2,1,0:T(8,128)(2,1)} async-done(((bf16[32,384,256]{2,1,0:T(8,128)(2,1)}), bf16[32,384,256]{2,1,0:T(8,128)(2,1)}, u32[]{:S(2)}, u32[]{:S(2)}) %all-to-all-start.4) | async-done | bytes 6291488 | tf_op jit(solution)/shard_map/all_to_all | solution.py:14
  387.0 9.0 %copy.19 = bf16[384,32,256]{2,1,0:T(8,128)(2,1)} copy(bf16[384,32,256]{2,0,1:T(8,128)(2,1)} %bitcast.34) | data formatting | bytes 12582912 | tf_op jit(solution)/shard_map/reshape | solution.py:14
  396.1 10.4 %reshape_reshape.17 = bf16[3,128,8192]{2,1,0:T(8,128)(2,1)} reshape(bf16[384,32,256]{2,1,0:T(8,128)(2,1)} %copy.19) | data formatting | bytes 12582912 | tf_op jit(solution)/shard_map/reshape;reshape | solution.py:59
  406.5 18.3 %while.52 = (s32[]{:T(128)}, f32[3,128,256]{2,1,0:T(8,128)S(1)}, bf16[3,128,8192]{2,1,0:T(8,128)(2,1)}, s32[3]{0:T(128)S(1)}, bf16[2,8192,256]{2,1,0:T(8,128)(2,1)}, /*index=5*/s32[]{:T(128)}, s32[]{:T(128)}, s32[]{:T(128)}) while((s32[]{:T(128)}, f32[3,128,256]{2,1,0:T(8,128)S(1)}, bf16[3,128,8192]{2,1,0:T(8,128)(2,1)}, s32[3]{0:T(128)S(1)}, ...), condition=%wide.region_24.27_spmd, body=%wide.region_23.26_spmd.sunk | while | flops 536870912 | bytes 6423687 | solution.py:68
  409.1 3.5 fusion.129
  415.2 3.5 fusion.129
  421.3 3.5 fusion.129
  426.5 8.6 %all-to-all-start.5 = ((f32[32,1,192]{2,1,0:T(1,128)}), f32[32,1,192]{2,1,0:T(1,128)S(1)}, u32[]{:S(2)}, u32[]{:S(2)}) async-start(f32[32,1,192]{2,1,0:T(1,128)} %broadcast_in_dim.153), calls=%async_computation.5 | async-start | bytes 65536 | tf_op jit(solution)/shard_map/all_to_all | solution.py:23
  436.5 6.1 all-to-all-done.5
  442.9 4.1 collective-permute-start.2
  448.7 2.1 gather_fusion.6
  450.9 3.4 stack.13
  454.3 5.8 all-to-all-start.6
  461.8 71.4 %all-to-all-done.6 = bf16[32,384,256]{2,1,0:T(8,128)(2,1)} async-done(((bf16[32,384,256]{2,1,0:T(8,128)(2,1)}), bf16[32,384,256]{2,1,0:T(8,128)(2,1)}, u32[]{:S(2)}, u32[]{:S(2)}) %all-to-all-start.6) | async-done | bytes 6291488 | tf_op jit(solution)/shard_map/all_to_all | solution.py:14
  533.2 9.0 %copy.21 = bf16[384,32,256]{2,1,0:T(8,128)(2,1)} copy(bf16[384,32,256]{2,0,1:T(8,128)(2,1)} %bitcast.39) | data formatting | bytes 12582912 | tf_op jit(solution)/shard_map/reshape | solution.py:14
  542.2 10.4 %reshape_reshape.18 = bf16[3,128,8192]{2,1,0:T(8,128)(2,1)} reshape(bf16[384,32,256]{2,1,0:T(8,128)(2,1)} %copy.21) | data formatting | bytes 12582912 | tf_op jit(solution)/shard_map/reshape;reshape | solution.py:59
  552.6 18.3 %while.53 = (s32[]{:T(128)}, f32[3,128,256]{2,1,0:T(8,128)S(1)}, bf16[3,128,8192]{2,1,0:T(8,128)(2,1)}, s32[3]{0:T(128)S(1)}, bf16[2,8192,256]{2,1,0:T(8,128)(2,1)}, /*index=5*/s32[]{:T(128)}, s32[]{:T(128)}, s32[]{:T(128)}) while((s32[]{:T(128)}, f32[3,128,256]{2,1,0:T(8,128)S(1)}, bf16[3,128,8192]{2,1,0:T(8,128)(2,1)}, s32[3]{0:T(128)S(1)}, ...), condition=%wide.region_33.36_spmd, body=%wide.region_32.35_spmd.sunk | while | flops 536870912 | bytes 6423687 | solution.py:68
  555.2 3.5 fusion.132
  561.3 3.5 fusion.132
  567.4 3.5 fusion.132
  572.6 8.8 %all-to-all-start.7 = ((f32[32,1,192]{2,1,0:T(1,128)}), f32[32,1,192]{2,1,0:T(1,128)S(1)}, u32[]{:S(2)}, u32[]{:S(2)}) async-start(f32[32,1,192]{2,1,0:T(1,128)} %broadcast_in_dim.156), calls=%async_computation.7 | async-start | bytes 65536 | tf_op jit(solution)/shard_map/all_to_all | solution.py:23
  582.7 6.1 all-to-all-done.7
  589.2 4.1 collective-permute-start.3
  594.9 2.1 gather_fusion.8
  597.2 3.4 stack.14
  600.5 6.2 all-to-all-start.8
  606.8 72.8 %all-to-all-done.8 = bf16[32,384,256]{2,1,0:T(8,128)(2,1)} async-done(((bf16[32,384,256]{2,1,0:T(8,128)(2,1)}), bf16[32,384,256]{2,1,0:T(8,128)(2,1)}, u32[]{:S(2)}, u32[]{:S(2)}) %all-to-all-start.8) | async-done | bytes 6291488 | tf_op jit(solution)/shard_map/all_to_all | solution.py:14
  679.6 9.0 %copy.23 = bf16[384,32,256]{2,1,0:T(8,128)(2,1)} copy(bf16[384,32,256]{2,0,1:T(8,128)(2,1)} %bitcast.45) | data formatting | bytes 12582912 | tf_op jit(solution)/shard_map/reshape | solution.py:14
  688.6 10.4 %reshape_reshape.19 = bf16[3,128,8192]{2,1,0:T(8,128)(2,1)} reshape(bf16[384,32,256]{2,1,0:T(8,128)(2,1)} %copy.23) | data formatting | bytes 12582912 | tf_op jit(solution)/shard_map/reshape;reshape | solution.py:59
  699.1 18.3 %while.54 = (s32[]{:T(128)}, f32[3,128,256]{2,1,0:T(8,128)S(1)}, bf16[3,128,8192]{2,1,0:T(8,128)(2,1)}, s32[3]{0:T(128)S(1)}, bf16[2,8192,256]{2,1,0:T(8,128)(2,1)}, /*index=5*/s32[]{:T(128)}, s32[]{:T(128)}, s32[]{:T(128)}) while((s32[]{:T(128)}, f32[3,128,256]{2,1,0:T(8,128)S(1)}, bf16[3,128,8192]{2,1,0:T(8,128)(2,1)}, s32[3]{0:T(128)S(1)}, ...), condition=%wide.region_42.45_spmd, body=%wide.region_41.44_spmd.sunk | while | flops 536870912 | bytes 6423687 | solution.py:68
  701.6 3.5 fusion.135
  707.7 3.5 fusion.135
  713.8 3.5 fusion.135
  719.1 8.6 %all-to-all-start.9 = ((f32[32,1,192]{2,1,0:T(1,128)}), f32[32,1,192]{2,1,0:T(1,128)S(1)}, u32[]{:S(2)}, u32[]{:S(2)}) async-start(f32[32,1,192]{2,1,0:T(1,128)} %broadcast_in_dim.160), calls=%async_computation.9 | async-start | bytes 65536 | tf_op jit(solution)/shard_map/all_to_all | solution.py:23
  727.8 7.3 all-to-all-done.9
  (150 shorter events, 46.1 us)
Async XLA Ops:
  12.8 82.6 %all-to-all-start = ((bf16[32,384,256]{2,1,0:T(8,128)(2,1)}), bf16[32,384,256]{2,1,0:T(8,128)(2,1)}, u32[]{:S(2)}, u32[]{:S(2)}) async-start(bf16[32,384,256]{2,1,0:T(8,128)(2,1)} %stack.10), calls=%async_computation | async-start | bytes 12582912 | tf_op jit(solution)/shard_map/all_to_all | solution.py:14
  114.8 41.2 %copy-start = (bf16[384,256]{1,0:T(8,128)(2,1)S(1)}, bf16[384,256]{1,0:T(8,128)(2,1)}, u32[]{:S(2)}) copy-start(bf16[384,256]{1,0:T(8,128)(2,1)} %param.17) | copy-start | bytes 589828
  134.9 16.1 %all-to-all-start.1 = ((f32[32,1,192]{2,1,0:T(1,128)}), f32[32,1,192]{2,1,0:T(1,128)S(1)}, u32[]{:S(2)}, u32[]{:S(2)}) async-start(f32[32,1,192]{2,1,0:T(1,128)} %broadcast_in_dim.147), calls=%async_computation.1 | async-start | bytes 65536 | tf_op jit(solution)/shard_map/all_to_all | solution.py:23
  151.3 4.7 collective-permute-start
  161.7 78.9 %all-to-all-start.2 = ((bf16[32,384,256]{2,1,0:T(8,128)(2,1)}), bf16[32,384,256]{2,1,0:T(8,128)(2,1)}, u32[]{:S(2)}, u32[]{:S(2)}) async-start(bf16[32,384,256]{2,1,0:T(8,128)(2,1)} %stack.11), calls=%async_computation.2 | async-start | bytes 12582912 | tf_op jit(solution)/shard_map/all_to_all | solution.py:14
  280.0 16.2 %all-to-all-start.3 = ((f32[32,1,192]{2,1,0:T(1,128)}), f32[32,1,192]{2,1,0:T(1,128)S(1)}, u32[]{:S(2)}, u32[]{:S(2)}) async-start(f32[32,1,192]{2,1,0:T(1,128)} %broadcast_in_dim.150), calls=%async_computation.3 | async-start | bytes 65536 | tf_op jit(solution)/shard_map/all_to_all | solution.py:23
  296.6 5.7 collective-permute-start.1
  307.9 79.1 %all-to-all-start.4 = ((bf16[32,384,256]{2,1,0:T(8,128)(2,1)}), bf16[32,384,256]{2,1,0:T(8,128)(2,1)}, u32[]{:S(2)}, u32[]{:S(2)}) async-start(bf16[32,384,256]{2,1,0:T(8,128)(2,1)} %stack.12), calls=%async_computation.4 | async-start | bytes 12582912 | tf_op jit(solution)/shard_map/all_to_all | solution.py:14
  426.5 16.0 %all-to-all-start.5 = ((f32[32,1,192]{2,1,0:T(1,128)}), f32[32,1,192]{2,1,0:T(1,128)S(1)}, u32[]{:S(2)}, u32[]{:S(2)}) async-start(f32[32,1,192]{2,1,0:T(1,128)} %broadcast_in_dim.153), calls=%async_computation.5 | async-start | bytes 65536 | tf_op jit(solution)/shard_map/all_to_all | solution.py:23
  442.9 5.7 collective-permute-start.2
  454.3 78.9 %all-to-all-start.6 = ((bf16[32,384,256]{2,1,0:T(8,128)(2,1)}), bf16[32,384,256]{2,1,0:T(8,128)(2,1)}, u32[]{:S(2)}, u32[]{:S(2)}) async-start(bf16[32,384,256]{2,1,0:T(8,128)(2,1)} %stack.13), calls=%async_computation.6 | async-start | bytes 12582912 | tf_op jit(solution)/shard_map/all_to_all | solution.py:14
  572.6 16.2 %all-to-all-start.7 = ((f32[32,1,192]{2,1,0:T(1,128)}), f32[32,1,192]{2,1,0:T(1,128)S(1)}, u32[]{:S(2)}, u32[]{:S(2)}) async-start(f32[32,1,192]{2,1,0:T(1,128)} %broadcast_in_dim.156), calls=%async_computation.7 | async-start | bytes 65536 | tf_op jit(solution)/shard_map/all_to_all | solution.py:23
  589.2 5.7 collective-permute-start.3
  600.5 79.1 %all-to-all-start.8 = ((bf16[32,384,256]{2,1,0:T(8,128)(2,1)}), bf16[32,384,256]{2,1,0:T(8,128)(2,1)}, u32[]{:S(2)}, u32[]{:S(2)}) async-start(bf16[32,384,256]{2,1,0:T(8,128)(2,1)} %stack.14), calls=%async_computation.8 | async-start | bytes 12582912 | tf_op jit(solution)/shard_map/all_to_all | solution.py:14
  719.1 16.0 %all-to-all-start.9 = ((f32[32,1,192]{2,1,0:T(1,128)}), f32[32,1,192]{2,1,0:T(1,128)S(1)}, u32[]{:S(2)}, u32[]{:S(2)}) async-start(f32[32,1,192]{2,1,0:T(1,128)} %broadcast_in_dim.160), calls=%async_computation.9 | async-start | bytes 65536 | tf_op jit(solution)/shard_map/all_to_all | solution.py:23
  735.4 0.6 copy-start.2
  736.0 0.7 copy-start.1
